TPU v7x, 256 devices: a whole 4x4x8 slice. The times are simulated.
256 devices in a mesh: batch: 4 (over z_lo, core), row: 4 (over x), col: 16 (over y, z_hi).
Axes of the slice: x: 4, y: 4, z: 8 (z_hi: 4, z_lo: 2; z = z_hi * 2 + z_lo), core: 2. Of those that a mesh axis runs over, the one named last changes fastest.
Arguments:
- embeddings: bfloat16 [512, 128, 512], P('batch', 'col', 'row'), may hold values from -170 to 170
- projection: bfloat16 [512, 32], replicated, may hold values from -0.25 to 0.25
- w_in: bfloat16 [16384, 2048], P('row', 'col'), may hold values from -0.046875 to 0.046875
- bias: float32 [2048], P('col'), may hold values from -3 to 3
- w_out: bfloat16 [2048, 128, 512], P(None, 'col', 'row'), may hold values from -0.125 to 0.125
- cotangent: bfloat16 [512, 128, 512], P('batch', 'col', 'row'), may hold values from -0.1796875 to 0.1796875
Outputs:
- mixed: bfloat16 [512, 128, 512], P('batch', 'col', 'row')
- grad_out: float32 [2048, 128, 512], P('batch', 'col', 'row')
- grad_in: float32 [16384, 2048], P('row', 'col')
- grad_bias: float32 [2048], P('col')
- grad_proj: float32 [512, 32], P('row')
All inputs are finite; a program needn't handle non-finite values.
Results may differ from a plain program's by a relative error of at most 0.006.
Values may be sent and summed in bfloat16 or wider, within the bound.
A program may use at most 128 MiB of HBM per device.

v0:
```python
import jax
import jax.numpy as jnp
from jax import lax
from jax.sharding import PartitionSpec as P

epsilon = 1e-06


def copy_for_each(array, axis):
    size = lax.axis_size(axis)
    return lax.all_to_all(
        jnp.broadcast_to(array[None], (size, *array.shape)), axis, 0, 0, tiled=True
    )


def of_everyone(array, axis):
    everything = copy_for_each(array, axis)
    return jnp.sum(everything, axis=0)


def joined_along(tiles, dim):
    tiles = jnp.moveaxis(tiles, 0, dim)
    lengths = tiles.shape
    return tiles.reshape(*lengths[:dim], lengths[dim] * lengths[dim + 1], *lengths[dim + 2 :])


def gathered_copies(array, axis, dim):
    return joined_along(copy_for_each(array, axis), dim)


def cut_along(array, dim, size):
    lengths = array.shape
    tiles = array.reshape(*lengths[:dim], size, lengths[dim] // size, *lengths[dim + 1 :])
    return jnp.moveaxis(tiles, dim, 0)


def sent_and_summed(array, axis, dim):
    size = lax.axis_size(axis)
    tiles = lax.all_to_all(cut_along(array, dim, size), axis, 0, 0, tiled=True)
    return jnp.sum(tiles, axis=0)


def in_one_piece(arrays, axis, dim, along):
    both = jnp.concatenate(arrays, axis=along)
    whole, at, gathered = (lax.all_gather(both, axis, axis=dim, tiled=True), 0, [])
    for a in arrays:
        gathered.append(lax.slice_in_dim(whole, at, at + a.shape[along], axis=along))
        at += a.shape[along]
    return tuple(gathered)


def filled_up(lines, size):
    spare = -lines.shape[0] % size
    if not spare:
        return lines
    return jnp.concatenate([lines, jnp.zeros((spare, *lines.shape[1:]), lines.dtype)])


def sum_by_parts(array, axis):
    lines = array.reshape(-1, *array.shape[1:][-1:])
    padded = filled_up(lines, lax.axis_size(axis))
    own = lax.psum_scatter(padded, axis, scatter_dimension=0, tiled=True)
    whole = lax.all_gather(own, axis, axis=0, tiled=True)
    return whole[: len(lines)].reshape(array.shape)


def contract_first(left, right):
    return lax.dot_general(
        left, right, (((0,), (0,)), ((), ())), preferred_element_type=jnp.float32
    )


def contract_last(left, right):
    return lax.dot_general(
        left, right, (((1,), (1,)), ((), ())), preferred_element_type=jnp.float32
    )


def local(embeddings, projection, w_in, bias, w_out, cotangent):
    highest = lax.Precision.HIGHEST
    tok_rows, feat_local, emb_local = embeddings.shape
    rank_cols = projection.shape[1]
    row_count = lax.axis_size("row")
    row_place = lax.axis_index("row")
    emb_float = embeddings.astype(jnp.float32)
    own_proj = lax.dynamic_slice_in_dim(projection, row_place * emb_local, emb_local, 0)
    folded = of_everyone(
        jnp.einsum("bde,ek->bdk", embeddings, own_proj, preferred_element_type=jnp.float32), "row"
    )
    partial_value = jnp.einsum("bde,bdk->bek", emb_float, folded, precision=highest)
    interact = lax.psum(partial_value, "col")
    feature_count = emb_local * row_count * rank_cols
    square_sum = of_everyone(jnp.sum(interact * interact, axis=(1, 2)), "row")
    inv_rms = lax.rsqrt(square_sum / feature_count + epsilon)[:, None, None]
    normed = interact * inv_rms
    activated = normed.astype(jnp.bfloat16).reshape(tok_rows, emb_local * rank_cols)
    preact = of_everyone(jnp.dot(activated, w_in, preferred_element_type=jnp.float32), "row") + bias
    hidden = jax.nn.silu(preact).astype(jnp.bfloat16)
    hidden_all = gathered_copies(hidden, "col", 1)
    flat_out = w_out.reshape(w_out.shape[0], feat_local * emb_local)
    mixed = (
        jnp.dot(hidden_all, flat_out, preferred_element_type=jnp.float32)
        .astype(jnp.bfloat16)
        .reshape(tok_rows, feat_local, emb_local)
    )
    cot_rows = cotangent.reshape(tok_rows, feat_local * emb_local)
    d_cols = sent_and_summed(contract_last(cot_rows, flat_out), "col", 1)
    d_hidden = of_everyone(d_cols, "row")
    sigmoid_pre = jax.nn.sigmoid(preact)
    d_preact = d_hidden * sigmoid_pre * (1.0 + preact * (1.0 - sigmoid_pre))
    d_pre_b = d_preact.astype(jnp.bfloat16)
    per_batch = w_out.shape[0] // lax.axis_size("batch")
    every_hidden, every_cot = in_one_piece((hidden_all, cot_rows), "batch", 0, 1)
    own_hidden = lax.dynamic_slice_in_dim(
        every_hidden, lax.axis_index("batch") * per_batch, per_batch, 1
    )
    grad_flat = contract_first(own_hidden, every_cot)
    grad_out = grad_flat.reshape(per_batch, feat_local, emb_local)
    grad_in, grad_bias = lax.psum(
        (contract_first(activated, d_pre_b), jnp.sum(d_preact, axis=0)), "batch"
    )
    d_act = sum_by_parts(contract_last(d_pre_b, w_in), "col").reshape(
        tok_rows, emb_local, rank_cols
    )
    inner_term = of_everyone(jnp.sum(d_act * normed, axis=(1, 2)), "row") / feature_count
    d_inter = (inv_rms * (d_act - normed * inner_term[:, None, None])).astype(jnp.bfloat16)
    back_fold = of_everyone(
        jnp.einsum("bek,bde->bdk", d_inter, embeddings, preferred_element_type=jnp.float32), "row"
    )
    grad_proj = of_everyone(
        jnp.einsum("bde,bdk->ek", emb_float, back_fold, precision=highest), ("batch", "col")
    )
    return (mixed, grad_out, grad_in, grad_bias, grad_proj)


def solution(mesh):
    placed = (
        P("batch", "col", "row"),
        P(),
        P("row", "col"),
        P("col"),
        P(None, "col", "row"),
        P("batch", "col", "row"),
    )
    return jax.shard_map(
        local,
        mesh=mesh,
        in_specs=placed,
        out_specs=(
            P("batch", "col", "row"),
            P("batch", "col", "row"),
            P("row", "col"),
            P("col"),
            P("row", None),
        ),
        check_vma=False,
    )
```

profile of v0, /device:TPU:1, one launch (start us, length us, event | category | flops | bytes accessed | tf_op | source)
XLA Modules:
  0.0 535.5 jit_solution(8240638500809765838)
XLA Ops:
  9.3 4.8 all-to-all-start
  14.4 7.4 %dot_general.47 = bf16[16,128,1024]{2,1,0:T(8,128)(2,1)} reshape(bf16[2048,8,128]{2,1,0:T(8,128)(2,1)} %param.10) | data formatting | bytes 8388608 | tf_op jit(solution)/shard_map/dot_general | solution.py:74
  22.1 3.2 convolution_bitcast_fusion.1
  25.3 4.7 convolution_bitcast_fusion.2
  30.0 11.6 %all-to-all-start.4 = ((f32[16,128,128]{2,1,0:T(8,128)}), f32[16,128,128]{2,1,0:T(8,128)}, u32[]{:S(2)}, u32[]{:S(2)}) async-start(f32[16,128,128]{2,1,0:T(8,128)} %convolution_bitcast_fusion.2), calls=%async_computation.4 | async-start | bytes 2097152 | tf_op jit(solution)/shard_map/all_to_all | solution.py:39
  41.6 172.1 %all-reduce.3.cloned.1.call-done = f32[128,128,32]{1,2,0:T(8,128)} async-done(((f32[128,128,32]{1,2,0:T(8,128)}), f32[128,128,32]{1,2,0:T(8,128)}) %all-reduce.3.cloned.1.call-update) | async-done | bytes 2097168 | tf_op jit(solution)/shard_map/psum | solution.py:91
  213.7 2.8 multiply_reduce_fusion.1
  217.0 3.3 all-to-all-start.1
  221.6 2.8 all-to-all-done.1
  225.1 4.0 all-to-all-start.5
  230.4 3.3 copy.58
  236.1 4.2 all-to-all-start.2
  241.3 5.8 %all-to-all-done.2 = f32[4,128,128]{2,1,0:T(8,128)} async-done(((f32[4,128,128]{2,1,0:T(8,128)}), f32[4,128,128]{2,1,0:T(8,128)}, u32[]{:S(2)}, u32[]{:S(2)}) %all-to-all-start.2) | async-done | bytes 262176 | tf_op jit(solution)/shard_map/all_to_all | solution.py:11
  249.6 1.8 fusion.15
  251.4 95.4 %reduce-scatter.2.cloned.1.call-done = f32[8,4096]{1,0:T(8,128)} async-done(((f32[128,4096]{1,0:T(8,128)}), f32[8,4096]{1,0:T(8,128)}) %reduce-scatter.2.cloned.1.call-update) | async-done | bytes 131088 | tf_op jit(solution)/shard_map/reduce_scatter | solution.py:62
  347.1 23.1 %all_to_all.47 = bf16[16,128,128]{1,2,0:T(8,128)(2,1)S(1)} all-to-all(bf16[16,128,128]{1,2,0:T(8,128)(2,1)S(1)} %broadcast_in_dim.19), channel_id=1, replica_groups=mesh['batch'=4,'row'=4,'col'=16] {'col'}, dimensions={0} | all-to-all | bytes 1048576 | tf_op jit(solution)/shard_map/all_to_all | solution.py:11
  371.0 1.9 pad_maximum_fusion
  372.9 34.7 %all-gather.5.cloned.1.call-done = f32[128,4096]{1,0:T(8,128)} async-done(((f32[8,4096]{1,0:T(8,128)}), f32[128,4096]{1,0:T(8,128)}) %all-gather.5.cloned.1.call-update) | async-done | bytes 2097168 | tf_op jit(solution)/shard_map/all_gather | solution.py:63
  407.6 2.9 copy.62
  410.5 3.4 copy.65
  413.9 3.5 multiply_reduce_fusion
  417.3 8.2 %all_to_all.48 = f32[4,1,128]{2,1,0:T(1,128)S(1)} all-to-all(f32[4,1,128]{2,1,0:T(1,128)S(1)} %broadcast_in_dim.21), channel_id=1, replica_groups=mesh['batch'=4,'row'=4,'col'=16] {'row'}, dimensions={0} | all-to-all | bytes 4096 | tf_op jit(solution)/shard_map/all_to_all | solution.py:11
  425.5 3.1 convolution_bitcast_fusion.3
  430.8 3.5 all-to-all-start.7
  436.2 5.1 all-to-all-done.7
  442.6 10.9 %all-to-all-start.8 = ((f32[64,128,32]{1,2,0:T(8,128)}), f32[64,128,32]{1,2,0:T(8,128)S(1)}, u32[]{:S(2)}, u32[]{:S(2)}) async-start(f32[64,128,32]{1,2,0:T(8,128)} %broadcast_in_dim.23), calls=%async_computation.9 | async-start | bytes 2097152 | tf_op jit(solution)/shard_map/all_to_all | solution.py:11
  453.6 33.7 %psum.23 = f32[128]{0:T(128)} all-reduce(f32[128]{0:T(128)S(1)} %get-tuple-element.5), channel_id=1, replica_groups=mesh['batch'=4,'row'=4,'col'=16] {'batch'}, use_global_device_ids=true, to_apply=%region_9.10 | all-reduce | flops 128 | bytes 1024 | tf_op jit(solution)/shard_map/psum | solution.py:119
  487.3 3.0 fusion.6
  492.6 2.0 convolution_bitcast_fusion
  494.6 1.8 copy.72
  497.1 28.8 %all-reduce.5.cloned.1.call-done = f32[4096,128]{1,0:T(8,128)} async-done(((f32[4096,128]{1,0:T(8,128)}), f32[4096,128]{1,0:T(8,128)}) %all-reduce.5.cloned.1.call-update) | async-done | bytes 2097168 | tf_op jit(solution)/shard_map/psum | solution.py:119
  525.9 3.0 copy.87
  (64 shorter events, 22.0 us)
Async XLA Ops:
  7.2 226.5 %copy-start = (bf16[4096,128]{1,0:T(8,128)(2,1)S(1)}, bf16[4096,128]{1,0:T(8,128)(2,1)}, u32[]{:S(2)}) copy-start(bf16[4096,128]{1,0:T(8,128)(2,1)} %param.8) | copy-start | bytes 3145732
  7.2 7.0 %copy-start.7 = (bf16[128,8,128]{2,1,0:T(8,128)(2,1)S(1)}, bf16[128,8,128]{2,1,0:T(8,128)(2,1)}, u32[]{:S(2)}) copy-start(bf16[128,8,128]{2,1,0:T(8,128)(2,1)} %param.11) | copy-start | bytes 786436
  9.3 12.5 %all-to-all-start = ((f32[4,128,8,32]{1,3,2,0:T(8,128)}), f32[4,128,8,32]{1,3,2,0:T(8,128)S(1)}, u32[]{:S(2)}, u32[]{:S(2)}) async-start(f32[4,128,8,32]{1,3,2,0:T(8,128)} %broadcast_in_dim.16), calls=%async_computation | async-start | bytes 1048576 | tf_op jit(solution)/shard_map/all_to_all | solution.py:11
  14.2 199.5 %all-reduce.3.cloned.1.call-start = ((), (), s32[]{:S(2)}) async-start(), calls=%async_computation.10 | async-start | bytes 4194304 | tf_op jit(solution)/shard_map/psum | solution.py:91
  14.4 10.9 %copy-start.4 = (bf16[128,8,128]{0,2,1:T(8,128)(2,1)}, bf16[128,8,128]{0,2,1:T(8,128)(2,1)S(1)}, u32[]{:S(2)}) copy-start(bf16[128,8,128]{0,2,1:T(8,128)(2,1)S(1)} %copy.60) | copy-start | bytes 786436
  14.4 7.7 %copy-start.3 = (bf16[128,8,128]{2,1,0:T(8,128)(2,1)S(1)}, bf16[128,8,128]{2,1,0:T(8,128)(2,1)}, u32[]{:S(2)}) copy-start(bf16[128,8,128]{2,1,0:T(8,128)(2,1)} %param.6) | copy-start | bytes 786436
  30.0 186.4 %all-to-all-start.4 = ((f32[16,128,128]{2,1,0:T(8,128)}), f32[16,128,128]{2,1,0:T(8,128)}, u32[]{:S(2)}, u32[]{:S(2)}) async-start(f32[16,128,128]{2,1,0:T(8,128)} %convolution_bitcast_fusion.2), calls=%async_computation.4 | async-start | bytes 2097152 | tf_op jit(solution)/shard_map/all_to_all | solution.py:39
  213.7 15.5 %copy-start.1 = (f32[128,128,32]{1,2,0:T(8,128)S(1)}, f32[128,128,32]{1,2,0:T(8,128)}, u32[]{:S(2)}) copy-start(f32[128,128,32]{1,2,0:T(8,128)} %all-reduce.3.cloned.1.call-done) | copy-start | bytes 6291460
  217.0 7.4 %all-to-all-start.1 = ((f32[4,1,128]{2,1,0:T(1,128)}), f32[4,1,128]{2,1,0:T(1,128)S(1)}, u32[]{:S(2)}, u32[]{:S(2)}) async-start(f32[4,1,128]{2,1,0:T(1,128)} %broadcast_in_dim.17), calls=%async_computation.1 | async-start | bytes 4096 | tf_op jit(solution)/shard_map/all_to_all | solution.py:11
  225.1 10.3 %all-to-all-start.5 = ((f32[4,128,128]{2,1,0:T(8,128)}), f32[4,128,128]{2,1,0:T(8,128)}, u32[]{:S(2)}, u32[]{:S(2)}) async-start(f32[4,128,128]{2,1,0:T(8,128)} %broadcast_in_dim.20), calls=%async_computation.5 | async-start | bytes 524288 | tf_op jit(solution)/shard_map/all_to_all | solution.py:11
  233.7 15.0 %copy-start.8 = (f32[128]{0:T(128)S(1)}, f32[128]{0:T(128)}, u32[]{:S(2)}) copy-start(f32[128]{0:T(128)} %param.9) | copy-start | bytes 1540
  236.1 10.9 %all-to-all-start.2 = ((f32[4,128,128]{2,1,0:T(8,128)}), f32[4,128,128]{2,1,0:T(8,128)}, u32[]{:S(2)}, u32[]{:S(2)}) async-start(f32[4,128,128]{2,1,0:T(8,128)} %broadcast_in_dim.18), calls=%async_computation.2 | async-start | bytes 524288 | tf_op jit(solution)/shard_map/all_to_all | solution.py:11
  240.3 106.5 %reduce-scatter.2.cloned.1.call-start = ((), (), s32[]{:S(2)}) async-start(), calls=%async_computation.13 | async-start | bytes 2228224 | tf_op jit(solution)/shard_map/reduce_scatter | solution.py:62
  251.4 156.3 %all-gather.5.cloned.1.call-start = ((), (), s32[]{:S(2)}) async-start(), calls=%async_computation.14 | async-start | bytes 2228224 | tf_op jit(solution)/shard_map/all_gather | solution.py:63
  346.9 144.2 %all-gather.3.cloned.1.call-start = ((), (), s32[]{:S(2)}) async-start(), calls=%async_computation.11 | async-start | bytes 3932160 | tf_op jit(solution)/shard_map/all_gather | solution.py:45
  370.2 0.8 copy-start.5
  428.7 5.7 %copy-start.2 = (bf16[128,128,32]{0,2,1:T(8,128)(2,1)S(1)}, bf16[128,128,32]{0,2,1:T(8,128)(2,1)}, u32[]{:S(2)}) copy-start(bf16[128,128,32]{0,2,1:T(8,128)(2,1)} %copy.58) | copy-start | bytes 3145732
  430.8 10.4 %all-to-all-start.7 = ((f32[4,128,8,32]{1,3,2,0:T(8,128)}), f32[4,128,8,32]{1,3,2,0:T(8,128)S(1)}, u32[]{:S(2)}, u32[]{:S(2)}) async-start(f32[4,128,8,32]{1,3,2,0:T(8,128)} %broadcast_in_dim.22), calls=%async_computation.8 | async-start | bytes 1048576 | tf_op jit(solution)/shard_map/all_to_all | solution.py:11
  434.3 91.6 %all-reduce.5.cloned.1.call-start = ((), (), s32[]{:S(2)}) async-start(), calls=%async_computation.12 | async-start | bytes 4194304 | tf_op jit(solution)/shard_map/psum | solution.py:119
  436.1 51.2 %copy-start.6 = (bf16[16,128,128]{1,2,0:T(8,128)(2,1)S(1)}, bf16[16,128,128]{1,2,0:T(8,128)(2,1)}, u32[]{:S(2)}) copy-start(bf16[16,128,128]{1,2,0:T(8,128)(2,1)} %copy-done.5) | copy-start | bytes 1572868
  442.6 53.8 %all-to-all-start.8 = ((f32[64,128,32]{1,2,0:T(8,128)}), f32[64,128,32]{1,2,0:T(8,128)S(1)}, u32[]{:S(2)}, u32[]{:S(2)}) async-start(f32[64,128,32]{1,2,0:T(8,128)} %broadcast_in_dim.23), calls=%async_computation.9 | async-start | bytes 2097152 | tf_op jit(solution)/shard_map/all_to_all | solution.py:11
  491.1 1.6 slice-start
Sparse Core Ops, SparseCore 0:
  25.4 188.1 all-reduce.2
  251.5 95.3 reduce-scatter.1
  349.3 58.3 all-gather.4
  409.3 39.9 all-gather.2
  452.4 73.5 all-reduce.4
where the time goes:
time: 537 us; the launch traced here: 536 us
  waiting for transfers between devices  345 us (64%)
  blocking collectives  65 us (12%)
  starting transfers between devices  42.5 us (8%)
  local copies, waits for them, and re-layouts  31.8 us (6%)
  matrix products  22.6 us (4%)
  other arithmetic  14.9 us (3%)
  between operations  14 us (3%)
    psum x1, waiting for transfers between devices, local(): interact = lax.psum(partial_value, 'col')  172 us
    reduce_scatter x1, waiting for transfers between devices, sum_by_parts(): own = lax.psum_scatter(padded, axis, scatter_dimension=0, tiled=True)  95.4 us
    all_gather x1, waiting for transfers between devices, sum_by_parts(): whole = lax.all_gather(own, axis, axis=0, tiled=True)  34.7 us
    psum x1, blocking collectives, local(): lax.psum((contract_first(activated, d_pre_b), jnp.sum(d_preact, axis=0)),...  33.7 us
    all_to_all x2, blocking collectives, copy_for_each(): lax.all_to_all(jnp.broadcast_to(array[None], (size, *array.shape)), axis,...  31.3 us
    all_to_all x6, starting transfers between devices, copy_for_each(): lax.all_to_all(jnp.broadcast_to(array[None], (size, *array.shape)), axis,...  30.8 us
    psum x1, waiting for transfers between devices, local(): lax.psum((contract_first(activated, d_pre_b), jnp.sum(d_preact, axis=0)),...  28.8 us
    all_to_all x6, waiting for transfers between devices, copy_for_each(): lax.all_to_all(jnp.broadcast_to(array[None], (size, *array.shape)), axis,...  13.6 us
  transfers between devices with their start and end apart: 12, of which 7 were waited for; matrix products, arithmetic and copies ran while one was open for 10% of the time, Pallas kernels for 0%

commit v1 on v0

--- a/solution.py
+++ b/solution.py
@@ -88,7 +88,7 @@
         jnp.einsum("bde,ek->bdk", embeddings, own_proj, preferred_element_type=jnp.float32), "row"
     )
     partial_value = jnp.einsum("bde,bdk->bek", emb_float, folded, precision=highest)
-    interact = lax.psum(partial_value, "col")
+    interact = jnp.sum(lax.all_gather(partial_value, "col"), axis=0)
     feature_count = emb_local * row_count * rank_cols
     square_sum = of_everyone(jnp.sum(interact * interact, axis=(1, 2)), "row")
     inv_rms = lax.rsqrt(square_sum / feature_count + epsilon)[:, None, None]

time: 537 us -> 748 us (1.39)
  waiting for transfers between devices: 345 us -> 551 us
  other arithmetic: 14.9 us -> 22.9 us
    all_gather x0 -> x1, waiting for transfers between devices: none -> 375 us  [local(): interact = jnp.sum(lax.all_gather(partial_value, 'col'), axis=0)]
    psum x1 -> x0, waiting for transfers between devices: 172 us -> none  [local(): interact = lax.psum(partial_value, 'col')]
    reduce_sum x0 -> x1, other arithmetic: none -> 12.7 us  [local(): interact = jnp.sum(lax.all_gather(partial_value, 'col'), axis=0)]
    psum x1, waiting for transfers between devices: 28.8 us -> 38.6 us  [local(): lax.psum((contract_first(activated, d_pre_b), jnp.sum(d_preact, axis=0)),...]
  transfers between devices with their start and end apart: 12 -> 12, of which waited for: 7 -> 7; matrix products, arithmetic and copies ran while one was open for 10% -> 8% of each run, Pallas kernels for 0% -> 0%
where the time goes in v1:
time: 748 us; the launch traced here: 747 us
  waiting for transfers between devices  551 us (74%)
  blocking collectives  62.7 us (8%)
  starting transfers between devices  42.2 us (6%)
  local copies, waits for them, and re-layouts  31.7 us (4%)
  other arithmetic  22.9 us (3%)
  matrix products  22.3 us (3%)
  between operations  14 us (2%)
    all_gather x1, waiting for transfers between devices, local(): interact = jnp.sum(lax.all_gather(partial_value, 'col'), axis=0)  375 us
    reduce_scatter x1, waiting for transfers between devices, sum_by_parts(): own = lax.psum_scatter(padded, axis, scatter_dimension=0, tiled=True)  88 us
    psum x1, waiting for transfers between devices, local(): lax.psum((contract_first(activated, d_pre_b), jnp.sum(d_preact, axis=0)),...  38.6 us
    all_gather x1, waiting for transfers between devices, sum_by_parts(): whole = lax.all_gather(own, axis, axis=0, tiled=True)  36.4 us
    all_to_all x2, blocking collectives, copy_for_each(): lax.all_to_all(jnp.broadcast_to(array[None], (size, *array.shape)), axis,...  36.2 us
    all_to_all x6, starting transfers between devices, copy_for_each(): lax.all_to_all(jnp.broadcast_to(array[None], (size, *array.shape)), axis,...  31.1 us
    psum x1, blocking collectives, local(): lax.psum((contract_first(activated, d_pre_b), jnp.sum(d_preact, axis=0)),...  26.5 us
  transfers between devices with their start and end apart: 12, of which 7 were waited for; matrix products, arithmetic and copies ran while one was open for 8% of the time, Pallas kernels for 0%

profile of v1, /device:TPU:1, one launch (start us, length us, event | category | flops | bytes accessed | tf_op | source)
XLA Modules:
  0.0 746.6 jit_solution(12240215444937441918)
XLA Ops:
  8.6 13.2 %all_to_all.47 = f32[4,128,8,32]{1,3,2,0:T(8,128)S(1)} all-to-all(f32[4,128,8,32]{1,3,2,0:T(8,128)S(1)} %broadcast_in_dim.16), channel_id=1, replica_groups=mesh['batch'=4,'row'=4,'col'=16] {'row'}, dimensions={0} | all-to-all | bytes 1048576 | tf_op jit(solution)/shard_map/all_to_all | solution.py:11
  22.1 3.2 convolution_bitcast_fusion.1
  25.6 7.4 dot_general.47
  33.0 4.7 convolution_bitcast_fusion.2
  37.6 11.0 %all-to-all-start.4 = ((f32[16,128,128]{2,1,0:T(8,128)}), f32[16,128,128]{2,1,0:T(8,128)}, u32[]{:S(2)}, u32[]{:S(2)}) async-start(f32[16,128,128]{2,1,0:T(8,128)} %convolution_bitcast_fusion.2), calls=%async_computation.4 | async-start | bytes 2097152 | tf_op jit(solution)/shard_map/all_to_all | solution.py:39
  48.6 374.5 %all-gather.9.cloned.1.call-done = f32[2048,128,32]{1,2,0:T(8,128)} async-done(((f32[128,128,32]{1,2,0:T(8,128)}), f32[2048,128,32]{1,2,0:T(8,128)}) %all-gather.9.cloned.1.call-update) | async-done | bytes 33554448 | tf_op jit(solution)/shard_map/all_gather | solution.py:91
  423.2 12.7 %reduce_sum.111 = f32[128,128,32]{1,2,0:T(8,128)S(1)} reduce(f32[16,128,128,32]{2,3,1,0:T(8,128)} %bitcast.51, f32[]{:T(128)} %constant.24.clone.1), dimensions={0}, to_apply=%region_1.0 | reduce | flops 7864320 | bytes 35651588 | tf_op jit(solution)/shard_map/reduce_sum | solution.py:91
  437.5 3.9 all-to-all-start.1
  442.7 2.2 copy.55
  445.0 2.9 copy.57
  448.6 4.2 all-to-all-start.5
  452.8 2.1 fusion.23
  454.9 3.5 all-to-all-done.5
  459.2 4.0 all-to-all-start.2
  464.2 4.6 all-to-all-done.2
  473.1 88.0 %reduce-scatter.2.cloned.1.call-done = f32[8,4096]{1,0:T(8,128)} async-done(((f32[128,4096]{1,0:T(8,128)}), f32[8,4096]{1,0:T(8,128)}) %reduce-scatter.2.cloned.1.call-update) | async-done | bytes 131088 | tf_op jit(solution)/shard_map/reduce_scatter | solution.py:62
  561.4 23.0 %all_to_all.48 = bf16[16,128,128]{1,2,0:T(8,128)(2,1)S(1)} all-to-all(bf16[16,128,128]{1,2,0:T(8,128)(2,1)S(1)} %broadcast_in_dim.19), channel_id=1, replica_groups=mesh['batch'=4,'row'=4,'col'=16] {'col'}, dimensions={0} | all-to-all | bytes 1048576 | tf_op jit(solution)/shard_map/all_to_all | solution.py:11
  585.4 36.4 %all-gather.7.cloned.1.call-done = f32[128,4096]{1,0:T(8,128)} async-done(((f32[8,4096]{1,0:T(8,128)}), f32[128,4096]{1,0:T(8,128)}) %all-gather.7.cloned.1.call-update) | async-done | bytes 2097168 | tf_op jit(solution)/shard_map/all_gather | solution.py:63
  621.8 2.6 multiply_reduce_fusion
  625.0 4.3 all-to-all-start.6
  629.2 2.9 copy.61
  632.1 3.4 copy.63
  635.5 2.4 convolution_bitcast_fusion.3
  639.0 4.2 all-to-all-start.7
  643.3 1.9 fusion.17
  645.2 5.0 all-to-all-done.7
  651.7 10.4 %all-to-all-start.8 = ((f32[64,128,32]{1,2,0:T(8,128)}), f32[64,128,32]{1,2,0:T(8,128)S(1)}, u32[]{:S(2)}, u32[]{:S(2)}) async-start(f32[64,128,32]{1,2,0:T(8,128)} %broadcast_in_dim.23), calls=%async_computation.9 | async-start | bytes 2097152 | tf_op jit(solution)/shard_map/all_to_all | solution.py:11
  662.1 26.5 %psum.15 = f32[128]{0:T(128)} all-reduce(f32[128]{0:T(128)S(1)} %get-tuple-element.5), channel_id=1, replica_groups=mesh['batch'=4,'row'=4,'col'=16] {'batch'}, use_global_device_ids=true, to_apply=%region_9.10 | all-reduce | flops 128 | bytes 1024 | tf_op jit(solution)/shard_map/psum | solution.py:119
  688.6 2.9 fusion.6
  693.9 2.0 convolution_bitcast_fusion
  698.4 38.6 %all-reduce.2.cloned.1.call-done = f32[4096,128]{1,0:T(8,128)} async-done(((f32[4096,128]{1,0:T(8,128)}), f32[4096,128]{1,0:T(8,128)}) %all-reduce.2.cloned.1.call-update) | async-done | bytes 2097168 | tf_op jit(solution)/shard_map/psum | solution.py:119
  737.0 3.1 copy.84
  (67 shorter events, 20.9 us)
Async XLA Ops:
  7.2 445.7 %copy-start = (bf16[4096,128]{1,0:T(8,128)(2,1)S(1)}, bf16[4096,128]{1,0:T(8,128)(2,1)}, u32[]{:S(2)}) copy-start(bf16[4096,128]{1,0:T(8,128)(2,1)} %param.8) | copy-start | bytes 3145732
  7.2 14.9 %copy-start.3 = (bf16[128,8,128]{2,1,0:T(8,128)(2,1)S(1)}, bf16[128,8,128]{2,1,0:T(8,128)(2,1)}, u32[]{:S(2)}) copy-start(bf16[128,8,128]{2,1,0:T(8,128)(2,1)} %param.6) | copy-start | bytes 786436
  7.2 416.0 %all-gather.9.cloned.1.call-start = ((), (), s32[]{:S(2)}) async-start(), calls=%async_computation.14 | async-start | bytes 35651584 | tf_op jit(solution)/shard_map/all_gather | solution.py:91
  22.1 3.2 copy-start.8
  25.5 7.4 copy-start.4
  37.6 399.3 %all-to-all-start.4 = ((f32[16,128,128]{2,1,0:T(8,128)}), f32[16,128,128]{2,1,0:T(8,128)}, u32[]{:S(2)}, u32[]{:S(2)}) async-start(f32[16,128,128]{2,1,0:T(8,128)} %convolution_bitcast_fusion.2), calls=%async_computation.4 | async-start | bytes 2097152 | tf_op jit(solution)/shard_map/all_to_all | solution.py:39
  437.5 10.3 %all-to-all-start.1 = ((f32[4,1,128]{2,1,0:T(1,128)}), f32[4,1,128]{2,1,0:T(1,128)S(1)}, u32[]{:S(2)}, u32[]{:S(2)}) async-start(f32[4,1,128]{2,1,0:T(1,128)} %broadcast_in_dim.17), calls=%async_computation.1 | async-start | bytes 4096 | tf_op jit(solution)/shard_map/all_to_all | solution.py:11
  448.6 9.9 %all-to-all-start.5 = ((f32[4,128,128]{2,1,0:T(8,128)}), f32[4,128,128]{2,1,0:T(8,128)}, u32[]{:S(2)}, u32[]{:S(2)}) async-start(f32[4,128,128]{2,1,0:T(8,128)} %broadcast_in_dim.20), calls=%async_computation.5 | async-start | bytes 524288 | tf_op jit(solution)/shard_map/all_to_all | solution.py:11
  452.8 17.6 %copy-start.9 = (f32[128]{0:T(128)S(1)}, f32[128]{0:T(128)}, u32[]{:S(2)}) copy-start(f32[128]{0:T(128)} %param.9) | copy-start | bytes 1540
  459.2 9.6 %all-to-all-start.2 = ((f32[4,128,128]{2,1,0:T(8,128)}), f32[4,128,128]{2,1,0:T(8,128)}, u32[]{:S(2)}, u32[]{:S(2)}) async-start(f32[4,128,128]{2,1,0:T(8,128)} %broadcast_in_dim.18), calls=%async_computation.2 | async-start | bytes 524288 | tf_op jit(solution)/shard_map/all_to_all | solution.py:11
  463.2 97.9 %reduce-scatter.2.cloned.1.call-start = ((), (), s32[]{:S(2)}) async-start(), calls=%async_computation.12 | async-start | bytes 2228224 | tf_op jit(solution)/shard_map/reduce_scatter | solution.py:62
  473.0 111.3 %copy-start.5 = (bf16[128,8,128]{0,2,1:T(8,128)(2,1)S(1)}, bf16[128,8,128]{0,2,1:T(8,128)(2,1)}, u32[]{:S(2)}) copy-start(bf16[128,8,128]{0,2,1:T(8,128)(2,1)} %copy-done.4) | copy-start | bytes 786436
  473.1 148.7 %all-gather.7.cloned.1.call-start = ((), (), s32[]{:S(2)}) async-start(), calls=%async_computation.13 | async-start | bytes 2228224 | tf_op jit(solution)/shard_map/all_gather | solution.py:63
  561.1 131.2 %all-gather.5.cloned.1.call-start = ((), (), s32[]{:S(2)}) async-start(), calls=%async_computation.10 | async-start | bytes 3932160 | tf_op jit(solution)/shard_map/all_gather | solution.py:45
  584.3 40.1 %copy-start.6 = (bf16[16,128,128]{1,2,0:T(8,128)(2,1)}, bf16[16,128,128]{1,2,0:T(8,128)(2,1)S(1)}, u32[]{:S(2)}) copy-start(bf16[16,128,128]{1,2,0:T(8,128)(2,1)S(1)} %all_to_all.48) | copy-start | bytes 1572868
  625.0 10.5 %all-to-all-start.6 = ((f32[4,1,128]{2,1,0:T(1,128)}), f32[4,1,128]{2,1,0:T(1,128)S(1)}, u32[]{:S(2)}, u32[]{:S(2)}) async-start(f32[4,1,128]{2,1,0:T(1,128)} %broadcast_in_dim.21), calls=%async_computation.7 | async-start | bytes 4096 | tf_op jit(solution)/shard_map/all_to_all | solution.py:11
  637.9 5.4 copy-start.2
  639.0 11.2 %all-to-all-start.7 = ((f32[4,128,8,32]{1,3,2,0:T(8,128)}), f32[4,128,8,32]{1,3,2,0:T(8,128)S(1)}, u32[]{:S(2)}, u32[]{:S(2)}) async-start(f32[4,128,8,32]{1,3,2,0:T(8,128)} %broadcast_in_dim.22), calls=%async_computation.8 | async-start | bytes 1048576 | tf_op jit(solution)/shard_map/all_to_all | solution.py:11
  643.3 93.7 %all-reduce.2.cloned.1.call-start = ((), (), s32[]{:S(2)}) async-start(), calls=%async_computation.11 | async-start | bytes 4194304 | tf_op jit(solution)/shard_map/psum | solution.py:119
  645.2 43.4 %copy-start.7 = (bf16[16,128,128]{1,2,0:T(8,128)(2,1)S(1)}, bf16[16,128,128]{1,2,0:T(8,128)(2,1)}, u32[]{:S(2)}) copy-start(bf16[16,128,128]{1,2,0:T(8,128)(2,1)} %copy-done.6) | copy-start | bytes 1572868
  651.7 46.0 %all-to-all-start.8 = ((f32[64,128,32]{1,2,0:T(8,128)}), f32[64,128,32]{1,2,0:T(8,128)S(1)}, u32[]{:S(2)}, u32[]{:S(2)}) async-start(f32[64,128,32]{1,2,0:T(8,128)} %broadcast_in_dim.23), calls=%async_computation.9 | async-start | bytes 2097152 | tf_op jit(solution)/shard_map/all_to_all | solution.py:11
  692.3 1.6 slice-start
  737.0 3.1 copy-start.1
Sparse Core Ops, SparseCore 0:
  25.4 397.7 all-gather.8
  473.2 87.8 reduce-scatter.1
  563.5 58.2 all-gather.6
  623.5 39.9 all-gather.4
  666.6 70.3 all-reduce.1
